TPU v7x, 512 devices: a whole 4x4x16 slice. The times are simulated.
512 devices in a mesh: pack: 16 (over y, x), seq: 32 (over z, core).
Axes of the slice: x: 4, y: 4, z: 16, core: 2. Of those that a mesh axis runs over, the one named last changes fastest.
Arguments:
- queries: bfloat16 [65536, 2048], P(('pack', 'seq')), parts along dimension 0, may hold values from -48 to 48
- token_key_heads: bfloat16 [65536, 256], P(('pack', 'seq')), parts along dimension 0, may hold values from -6 to 6
- token_value_heads: bfloat16 [65536, 256], P(('pack', 'seq')), parts along dimension 0, may hold values from -6 to 6
- residual: bfloat16 [65536, 1024], P(('pack', 'seq')), parts along dimension 0, may hold values from -40 to 40
- out_weight: bfloat16 [2048, 1024], P('seq'), may hold values from -0.125 to 0.125
- norm_gain: bfloat16 [1024], replicated, may hold values from 0.5 to 1.5
- w_gate: bfloat16 [32, 1024, 384], P('seq'), may hold values from -0.1875 to 0.1875
- w_up: bfloat16 [32, 1024, 384], P('seq'), may hold values from -0.1875 to 0.1875
- w_down: bfloat16 [32, 384, 1024], P('seq'), may hold values from -0.3125 to 0.3125
- expert_ids: int32 [65536, 8], P(('pack', 'seq')), parts along dimension 0, may hold values from 0 to 31, all different within a row; in each aligned block of 128 rows (0 to 127, 128 to 255, ...) at most 48 rows name the same one
- gate_weights: float32 [65536, 8], P(('pack', 'seq')), parts along dimension 0, may hold values from 0.05 to 0.3
- doc_of_block: int32 [512], P('pack'), parts along dimension 0, may hold values from 0 to 7, never falling along the last dimension, each value on 1 to 8 neighbouring positions
Outputs:
- attention: bfloat16 [65536, 2048], P(('pack', 'seq')), parts along dimension 0
- hidden_out: bfloat16 [65536, 1024], P(('pack', 'seq')), parts along dimension 0
- expert_mix: bfloat16 [65536, 1024], P(('pack', 'seq')), parts along dimension 0
There are 16 independent parts, one for each index of `pack`. A program takes and returns all parts, laid end to end along the dimension named above; an argument that names none is the same for every part. Nothing has to cross between parts.
Inputs may be any that keep to these rules, and one draw needn't show every extreme that they name: `expert_ids`: each row names 8 different experts; within the rows of one block no expert is named more than 48 times, and in every draw some expert is named exactly 48 times by the rows of some block. `doc_of_block`: never falls from block to block; each document covers 1 to 8 blocks, one exactly 8.
All inputs are finite; a program needn't handle non-finite values.
Results may differ from a plain program's by a relative error of at most 0.015.
Values may be sent and summed in bfloat16 or wider, within the bound.
A program may use at most 64 MiB of HBM per device.

v0:
```python
import math
import jax
import jax.numpy as jnp
from jax import lax
from jax.sharding import PartitionSpec as P

QUERY_HEADS = 16
KEY_VALUE_HEADS = 2
HEAD_SIZE = 128
TOP = 8


def attend(queries, key_token_rows, value_token_rows, query_pos, key_pos, allowed):
    token_rows = queries.shape[0]
    heads_per_group = QUERY_HEADS // KEY_VALUE_HEADS
    token_query_heads = queries.reshape(token_rows, KEY_VALUE_HEADS, heads_per_group, HEAD_SIZE)
    key_count = key_token_rows.shape[0]
    tile_length = math.gcd(key_count, 512)
    number_of_tiles = key_count // tile_length
    key_tile_list = key_token_rows.reshape(number_of_tiles, tile_length, KEY_VALUE_HEADS, HEAD_SIZE)
    value_tile_list = value_token_rows.reshape(
        number_of_tiles, tile_length, KEY_VALUE_HEADS, HEAD_SIZE
    )
    pos_tiles = key_pos.reshape(number_of_tiles, tile_length)
    allowed_tiles = allowed.reshape(number_of_tiles, tile_length)
    factor = 1.0 / HEAD_SIZE**0.5

    def tile_step(running, tile):
        key_tile, value_tile, pos_tile, allowed_tile = tile
        visible = allowed_tile[None, :] & (pos_tile[None, :] <= query_pos[:, None])

        def compute(current):
            run_max, run_sum, accum = current
            scores = (
                jnp.einsum(
                    "tkgd,skd->kgts",
                    token_query_heads,
                    key_tile,
                    preferred_element_type=jnp.float32,
                )
                * factor
            )
            scores = jnp.where(visible, scores, -1e30)
            new_max = jnp.maximum(run_max, jnp.max(scores, axis=-1))
            terms = jnp.where(visible, jnp.exp(scores - new_max[..., None]), 0.0)
            rescale = jnp.exp(run_max - new_max)
            new_sum = run_sum * rescale + jnp.sum(terms, axis=-1)
            product = jnp.einsum(
                "kgts,skd->kgtd",
                terms.astype(jnp.bfloat16),
                value_tile,
                preferred_element_type=jnp.float32,
            )
            return (new_max, new_sum, accum * rescale[..., None] + product)

        return (lax.cond(jnp.any(visible), compute, lambda current: current, running), None)

    start_state = (
        jnp.full((KEY_VALUE_HEADS, heads_per_group, token_rows), -1e30, jnp.float32),
        jnp.zeros((KEY_VALUE_HEADS, heads_per_group, token_rows), jnp.float32),
        jnp.zeros((KEY_VALUE_HEADS, heads_per_group, token_rows, HEAD_SIZE), jnp.float32),
    )
    final_state, _ = lax.scan(
        tile_step, start_state, (key_tile_list, value_tile_list, pos_tiles, allowed_tiles)
    )
    run_max, run_sum, accum = final_state
    result = accum / run_sum[..., None]
    return (
        jnp.transpose(result, (2, 0, 1, 3))
        .reshape(token_rows, QUERY_HEADS * HEAD_SIZE)
        .astype(jnp.bfloat16)
    )


def expert_rows(arrived, gate_proj, up_proj, down_proj):
    sources, slot_count, width = arrived.shape
    flat_rows = arrived.reshape(sources * slot_count, width)
    gate_part = jnp.dot(flat_rows, gate_proj, preferred_element_type=jnp.float32)
    up_part = jnp.dot(flat_rows, up_proj, preferred_element_type=jnp.float32)
    activated = (jax.nn.silu(gate_part) * up_part).astype(jnp.bfloat16)
    produced = jnp.dot(activated, down_proj, preferred_element_type=jnp.float32).astype(
        jnp.bfloat16
    )
    return produced.reshape(sources, slot_count, width)


def shards(
    queries,
    token_key_heads,
    token_value_heads,
    residual,
    out_weight,
    norm_gain,
    w_gate,
    w_up,
    w_down,
    expert_ids,
    gate_weights,
    doc_of_block,
):
    token_rows = queries.shape[0]
    blocks = lax.axis_size("seq")
    own_index = lax.axis_index("seq")
    local_pos = jnp.arange(token_rows, dtype=jnp.int32)
    query_pos = own_index * token_rows + local_pos
    own_doc = doc_of_block[own_index]
    key_head_width = token_key_heads.shape[1]
    key_token_rows, value_token_rows = (
        lax.all_gather(token_key_heads, "seq", axis=0, tiled=True),
        lax.all_gather(token_value_heads, "seq", axis=0, tiled=True),
    )
    key_pos = jnp.arange(blocks * token_rows, dtype=jnp.int32)
    key_block = key_pos // token_rows
    allowed = (key_block <= own_index) & ((doc_of_block[key_block] == own_doc) | (key_block == 0))
    key_token_rows = key_token_rows.reshape(
        key_token_rows.shape[0], KEY_VALUE_HEADS, key_head_width // KEY_VALUE_HEADS
    )
    value_token_rows = value_token_rows.reshape(
        value_token_rows.shape[0], KEY_VALUE_HEADS, key_head_width // KEY_VALUE_HEADS
    )
    attention = attend(queries, key_token_rows, value_token_rows, query_pos, key_pos, allowed)
    width = residual.shape[1]
    projected = jnp.dot(
        attention,
        lax.all_gather(out_weight, "seq", axis=0, tiled=True),
        preferred_element_type=jnp.float32,
    )
    hidden_state = residual.astype(jnp.float32) + projected
    mean_square = jnp.mean(hidden_state * hidden_state, axis=-1, keepdims=True)
    normed = (hidden_state * lax.rsqrt(mean_square + 1e-06) * norm_gain.astype(jnp.float32)).astype(
        jnp.bfloat16
    )
    slot_cap = min(token_rows, 3 * token_rows * TOP // (2 * blocks))
    routed_ids = expert_ids.reshape(-1)
    one_hot = (routed_ids[:, None] == jnp.arange(blocks, dtype=jnp.int32)[None, :]).astype(
        jnp.int32
    )
    earlier = jnp.cumsum(one_hot, axis=0) - one_hot
    slot_pos = jnp.sum(earlier * one_hot, axis=1)
    slot_index = routed_ids * slot_cap + slot_pos
    token_of = jnp.arange(token_rows * TOP, dtype=jnp.int32) // TOP
    outgoing = (
        jnp.zeros((blocks * slot_cap, width), jnp.bfloat16).at[slot_index].set(normed[token_of])
    )
    outgoing = outgoing.reshape(blocks, slot_cap, width)
    arrived = lax.all_to_all(outgoing, "seq", split_axis=0, concat_axis=0, tiled=True)
    served = expert_rows(arrived, w_gate[0], w_up[0], w_down[0])
    returned_rows = lax.all_to_all(served, "seq", split_axis=0, concat_axis=0, tiled=True)
    picked = returned_rows.reshape(blocks * slot_cap, width)[slot_index].astype(jnp.float32)
    weighted = picked * gate_weights.reshape(-1)[:, None]
    expert_mix = jnp.sum(weighted.reshape(token_rows, TOP, width), axis=1).astype(jnp.bfloat16)
    return (attention, hidden_state.astype(jnp.bfloat16), expert_mix)


def solution(mesh):
    in_specs = (
        P(("pack", "seq"), None),
        P(("pack", "seq"), None),
        P(("pack", "seq"), None),
        P(("pack", "seq"), None),
        P("seq", None),
        P(),
        P("seq", None, None),
        P("seq", None, None),
        P("seq", None, None),
        P(("pack", "seq"), None),
        P(("pack", "seq"), None),
        P("pack"),
    )
    out_specs = (P(("pack", "seq"), None), P(("pack", "seq"), None), P(("pack", "seq"), None))
    return jax.shard_map(shards, mesh=mesh, in_specs=in_specs, out_specs=out_specs, check_vma=False)
```

profile of v0, /device:TPU:4, one launch (start us, length us, event | category | flops | bytes accessed | tf_op | source)
XLA Modules:
  0.0 583.3 jit_solution(16247242193508925619)
XLA Ops:
  11.9 1.9 fusion.43
  13.8 2.1 fusion.42
  15.8 4.5 compare_select_fusion.1
  20.3 16.1 %select_compare_fusion = pred[4096]{0:T(1024)(128)(4,1)S(1)} fusion(pred[4096]{0:T(1024)(128)(4,1)S(1)} %compare_reduce_fusion, pred[4096]{0:T(1024)(128)(4,1)S(1)} %compare_reduce_fusion.1, pred[4096]{0:T(1024)(128)(4,1)S(1)} %compare_reduce_fusion.2, pred[4096]{0:T(1024)(128)(4,1)S(1)} %compare_reduce_fusion.3, ...), kind=kLoop, calls=%fused_computation.99 | loop fusion | flops 106496 | bytes 122984 | tf_op jit(solution)/shard_map/eq | solution.py:114
  36.4 1.3 copy.20
  38.8 9.0 %reduce-window.6 = s32[32,8,128]{2,1,0:T(8,128)S(1)} reduce-window(s32[32,8,128]{2,1,0:T(8,128)S(1)} %fusion.37, s32[]{:T(128)} %copy.62), window={size=1x1x128 pad=0_0x0_0x127_0}, to_apply=%region_7.8 | reduce-window | flops 4161536 | bytes 262148 | tf_op jit(solution)/shard_map/reduce-window
  48.6 37.9 %all-gather.4.cloned.1.call-done = bf16[4096,256]{1,0:T(8,128)(2,1)} async-done(((bf16[128,256]{1,0:T(8,128)(2,1)}), bf16[4096,256]{1,0:T(8,128)(2,1)}) %all-gather.4.cloned.1.call-update) | async-done | bytes 2097168 | tf_op jit(solution)/shard_map/all_gather | solution.py:109
  86.5 2.5 reshape.356
  89.0 1.8 copy.22
  90.8 66.5 %all-gather.6.cloned.1.call-done = bf16[4096,256]{1,0:T(8,128)(2,1)} async-done(((bf16[128,256]{1,0:T(8,128)(2,1)}), bf16[4096,256]{1,0:T(8,128)(2,1)}) %all-gather.6.cloned.1.call-update) | async-done | bytes 2097168 | tf_op jit(solution)/shard_map/all_gather | solution.py:110
  157.3 2.5 reshape.357
  159.9 1.8 copy.24
  161.7 18.0 %while.15 = (s32[]{:T(128)}, f32[2,8,128]{2,1,0:T(8,128)S(1)}, f32[2,8,128]{2,1,0:T(8,128)S(1)}, f32[2,8,128,128]{3,2,1,0:T(8,128)S(1)}, pred[8,512]{1,0:T(8,128...) while((s32[]{:T(128)}, f32[2,8,128]{2,1,0:T(8,128)S(1)}, ...), condition=%wide.region_6.7_spmd.clone, body=%wide.region_0.6_spmd.clone.sunk | while | flops 551227520 | bytes 16131831 | solution.py:63
  161.8 0.8 compare_and_fusion.2
  163.3 5.4 conditional.3
  163.3 1.7 fusion.2
  165.0 1.0 fusion.4
  166.0 2.6 fusion.8
  168.8 0.8 compare_and_fusion.2
  170.4 0.8 compare_and_fusion.2
  176.7 0.8 compare_and_fusion.2
  180.7 49.5 %all-gather.8.cloned.1.call-done = bf16[2048,1024]{1,0:T(8,128)(2,1)} async-done(((bf16[64,1024]{1,0:T(8,128)(2,1)}), bf16[2048,1024]{1,0:T(8,128)(2,1)}) %all-gather.8.cloned.1.call-update) | async-done | bytes 4194320 | tf_op jit(solution)/shard_map/all_gather | solution.py:125
  230.1 3.0 multiply_reduce_fusion
  233.9 14.9 %scatter_custom_fusion = bf16[1536,1024]{1,0:T(8,128)(2,1)} fusion(s32[1024]{0:T(1024)S(1)} %bitcast.128, bf16[128,1024]{1,0:T(8,128)(2,1)S(1)} %get-tuple-element.196, s32[1024]{0:T(1024)S(1)} %broadcast_clamp_fusion.1, bf16[]{:T(256)} %constant.107.clone.1), kind=kCustom, calls=%fused_computation.34 | custom fusion | bytes 3145730 | tf_op jit(solution)/shard_map/scatter | solution.py:143
  248.9 154.5 %all_to_all.10 = bf16[32,48,1024]{2,1,0:T(8,128)(2,1)S(1)} all-to-all(bf16[32,48,1024]{2,1,0:T(8,128)(2,1)} %bitcast.115), channel_id=1, replica_groups=mesh['pack'=16,'seq'=32] {'seq'}, dimensions={0} | all-to-all | bytes 6291456 | tf_op jit(solution)/shard_map/all_to_all | solution.py:146
  403.4 1.7 copy-done.1
  405.1 3.2 fusion.31
  408.3 7.8 %convolution_convert_fusion = bf16[1536,1024]{1,0:T(8,128)(2,1)} fusion(bf16[1536,1024]{1,0:T(8,128)(2,1)} %bitcast.118, f32[1536,384]{1,0:T(8,128)} %fusion.31, bf16[1,384,1024]{2,1,0:T(8,128)(2,1)S(1)} %copy-done, bf16[1,1024,384]{2,1,0:T(8,128)(2,1)S(1)} %copy-done.7), kind=kOutput, calls=%fused_computation.31 | convolution fusion | flops 2421030912 | bytes 10223616 | tf_op jit(solution)/shard_map/dot_general | solution.py:81
  416.1 4.9 all-to-all-start.1
  421.2 146.3 %all-to-all-done.1 = bf16[32,48,1024]{2,1,0:T(8,128)(2,1)} async-done(((bf16[32,48,1024]{2,1,0:T(8,128)(2,1)}), bf16[32,48,1024]{2,1,0:T(8,128)(2,1)}, u32[]{:S(2)}, u32[]{:S(2)}) %all-to-all-start.1) | async-done | bytes 3145760 | tf_op jit(solution)/shard_map/all_to_all | solution.py:148
  567.5 7.3 %gather_fusion = bf16[1024,1024]{1,0:T(8,128)(2,1)S(1)} fusion(bf16[1536,1024]{1,0:T(8,128)(2,1)} %bitcast.54, s32[1024]{0:T(1024)S(1)} %broadcast_clamp_fusion), kind=kCustom, calls=%fused_computation.1 | custom fusion | bytes 4198400 | tf_op jit(solution)/shard_map/gather | solution.py:149
  574.8 2.0 fusion.22
  (116 shorter events, 11.9 us)
Async XLA Ops:
  7.2 401.2 %copy-start = (bf16[1,384,1024]{2,1,0:T(8,128)(2,1)S(1)}, bf16[1,384,1024]{2,1,0:T(8,128)(2,1)}, u32[]{:S(2)}) copy-start(bf16[1,384,1024]{2,1,0:T(8,128)(2,1)} %param.24) | copy-start | bytes 2359300
  7.2 40.9 %copy-start.4 = (s32[128,8]{0,1:T(8,128)S(1)}, s32[128,8]{0,1:T(8,128)}, u32[]{:S(2)}) copy-start(s32[128,8]{0,1:T(8,128)} %param.25) | copy-start | bytes 12292
  7.2 79.3 %all-gather.4.cloned.1.call-start = ((), (), s32[]{:S(2)}) async-start(), calls=%async_computation.2 | async-start | bytes 2162688 | tf_op jit(solution)/shard_map/all_gather | solution.py:109
  7.9 149.4 %all-gather.6.cloned.1.call-start = ((), (), s32[]{:S(2)}) async-start(), calls=%async_computation.3 | async-start | bytes 2162688 | tf_op jit(solution)/shard_map/all_gather | solution.py:110
  8.7 221.5 %all-gather.8.cloned.1.call-start = ((), (), s32[]{:S(2)}) async-start(), calls=%async_computation.4 | async-start | bytes 4325376 | tf_op jit(solution)/shard_map/all_gather | solution.py:125
  179.8 50.4 %copy-start.3 = (bf16[128,1024]{1,0:T(8,128)(2,1)S(1)}, bf16[128,1024]{1,0:T(8,128)(2,1)}, u32[]{:S(2)}) copy-start(bf16[128,1024]{1,0:T(8,128)(2,1)} %param.19) | copy-start | bytes 786436
  180.6 53.3 %copy-start.2 = (bf16[16,8,16,128]{3,1,2,0:T(8,128)(2,1)}, bf16[16,8,16,128]{3,1,2,0:T(8,128)(2,1)S(1)}, u32[]{:S(2)}) copy-start(bf16[16,8,16,128]{3,1,2,0:T(8,128)(2,1)S(1)} %copy.43) | copy-start | bytes 1572868
  248.9 156.2 %copy-start.6 = (bf16[1,1024,384]{2,1,0:T(8,128)(2,1)S(1)}, bf16[1,1024,384]{2,1,0:T(8,128)(2,1)}, u32[]{:S(2)}) copy-start(bf16[1,1024,384]{2,1,0:T(8,128)(2,1)} %param.22) | copy-start | bytes 2359300
  403.4 1.7 copy-start.1
  405.1 3.3 copy-start.7
  416.1 5.0 copy-start.5
  416.1 151.3 %all-to-all-start.1 = ((bf16[32,48,1024]{2,1,0:T(8,128)(2,1)}), bf16[32,48,1024]{2,1,0:T(8,128)(2,1)}, u32[]{:S(2)}, u32[]{:S(2)}) async-start(bf16[32,48,1024]{2,1,0:T(8,128)(2,1)} %bitcast.116), calls=%async_computation.1 | async-start | bytes 6291456 | tf_op jit(solution)/shard_map/all_to_all | solution.py:148
Sparse Core Ops, SparseCore 0:
  10.1 76.2 all-gather.3
  88.6 68.6 all-gather.5
  159.4 70.6 all-gather.7
where the time goes:
time: 584 us; the launch traced here: 583 us
  waiting for transfers between devices  302 us (52%)
  blocking collectives  155 us (27%)
  other arithmetic  42.8 us (7%)
  local copies, waits for them, and re-layouts  40.6 us (7%)
  matrix products  18.4 us (3%)
  between operations  14 us (2%)
    all_to_all x1, blocking collectives, shards(): lax.all_to_all(outgoing, 'seq', split_axis=0, concat_axis=0, tiled=True)  155 us
    all_to_all x1, waiting for transfers between devices, shards(): lax.all_to_all(served, 'seq', split_axis=0, concat_axis=0, tiled=True)  146 us
    all_gather x1, waiting for transfers between devices, shards(): lax.all_gather(token_value_heads, 'seq', axis=0, tiled=True)  66.5 us
    all_gather x1, waiting for transfers between devices, shards(): lax.all_gather(out_weight, 'seq', axis=0, tiled=True)  49.5 us
    all_gather x1, waiting for transfers between devices, shards(): lax.all_gather(token_key_heads, 'seq', axis=0, tiled=True)  37.9 us
    eq x1, other arithmetic, shards(): doc_of_block[key_block] == own_doc  16.1 us
    scatter x1, local copies, waits for them, and re-layouts, shards(): jnp.zeros((blocks * slot_cap, width), jnp.bfloat16).at[slot_index]  14.9 us
  transfers between devices with their start and end apart: 4, of which 4 were waited for; matrix products, arithmetic and copies ran while one was open for 10% of the time, Pallas kernels for 0%

commit v1 on v0

--- a/solution.py
+++ b/solution.py
@@ -8,6 +8,13 @@
 KEY_VALUE_HEADS = 2
 HEAD_SIZE = 128
 TOP = 8
+
+
+def proceed_zone(slab_in):
+    a_now = jnp.stack([slab_in for _ in range(lax.psum(1, "seq"))], axis=0)
+    newest = lax.all_to_all(a_now, "seq", 0, 0)
+    passed = jnp.concatenate(newest, axis=0)
+    return passed
 
 
 def attend(queries, key_token_rows, value_token_rows, query_pos, key_pos, allowed):
@@ -107,7 +114,7 @@
     key_head_width = token_key_heads.shape[1]
     key_token_rows, value_token_rows = (
         lax.all_gather(token_key_heads, "seq", axis=0, tiled=True),
-        lax.all_gather(token_value_heads, "seq", axis=0, tiled=True),
+        proceed_zone(token_value_heads),
     )
     key_pos = jnp.arange(blocks * token_rows, dtype=jnp.int32)
     key_block = key_pos // token_rows

time: 584 us -> 561 us (0.961)
  waiting for transfers between devices: 302 us -> 230 us
  local copies, waits for them, and re-layouts: 40.6 us -> 60.9 us
  starting transfers between devices: 5.06 us -> 20.6 us
  other arithmetic: 42.8 us -> 54 us
    all_gather x1 -> x0, waiting for transfers between devices: 66.5 us -> none  [shards(): lax.all_gather(token_value_heads, 'seq', axis=0, tiled=True)]
    all_to_all x0 -> x1, starting transfers between devices: none -> 15.6 us  [proceed_zone(): newest = lax.all_to_all(a_now, 'seq', 0, 0)]
    all_gather x1, waiting for transfers between devices: 49.5 us -> 35.4 us  [shards(): lax.all_gather(out_weight, 'seq', axis=0, tiled=True)]
    another operation x3, other arithmetic: 9.14 us -> 15.8 us
    all_to_all x0 -> x1, waiting for transfers between devices: none -> 6.13 us  [proceed_zone(): newest = lax.all_to_all(a_now, 'seq', 0, 0)]
    unnamed x23 -> x32, local copies, waits for them, and re-layouts: 7.9 us -> 11.7 us
  transfers between devices with their start and end apart: 4 -> 4, of which waited for: 4 -> 4; matrix products, arithmetic and copies ran while one was open for 10% -> 17% of each run, Pallas kernels for 0% -> 0%
where the time goes in v1:
time: 561 us; the launch traced here: 558 us
  waiting for transfers between devices  230 us (41%)
  blocking collectives  154 us (27%)
  local copies, waits for them, and re-layouts  60.9 us (11%)
  other arithmetic  54 us (10%)
  starting transfers between devices  20.6 us (4%)
  matrix products  18.4 us (3%)
  between operations  14.3 us (3%)
    all_to_all x1, blocking collectives, shards(): lax.all_to_all(outgoing, 'seq', split_axis=0, concat_axis=0, tiled=True)  154 us
    all_to_all x1, waiting for transfers between devices, shards(): lax.all_to_all(served, 'seq', split_axis=0, concat_axis=0, tiled=True)  146 us
    all_gather x1, waiting for transfers between devices, shards(): lax.all_gather(token_key_heads, 'seq', axis=0, tiled=True)  41.2 us
    all_gather x1, waiting for transfers between devices, shards(): lax.all_gather(out_weight, 'seq', axis=0, tiled=True)  35.4 us
    eq x1, other arithmetic, shards(): doc_of_block[key_block] == own_doc  16.2 us
    another operation x3, other arithmetic  15.8 us
    all_to_all x1, starting transfers between devices, proceed_zone(): newest = lax.all_to_all(a_now, 'seq', 0, 0)  15.6 us
    scatter x1, local copies, waits for them, and re-layouts, shards(): jnp.zeros((blocks * slot_cap, width), jnp.bfloat16).at[slot_index]  14.9 us
  transfers between devices with their start and end apart: 4, of which 4 were waited for; matrix products, arithmetic and copies ran while one was open for 17% of the time, Pallas kernels for 0%

profile of v1, /device:TPU:4, one launch (start us, length us, event | category | flops | bytes accessed | tf_op | source)
XLA Modules:
  0.0 558.2 jit_solution(9408962357878951327)
XLA Ops:
  8.9 1.8 stack.2
  10.7 15.6 %all-to-all-start = ((bf16[32,128,256]{1,2,0:T(8,128)(2,1)}), bf16[32,128,256]{1,2,0:T(8,128)(2,1)S(1)}, u32[]{:S(2)}, u32[]{:S(2)}) async-start(bf16[32,128,256]{1,2,0:T(8,128)(2,1)} %stack.2), calls=%async_computation | async-start | bytes 4194304 | tf_op jit(solution)/shard_map/all_to_all | solution.py:15
  30.9 4.5 compare_select_fusion.1
  35.3 16.2 %select_compare_fusion = pred[4096]{0:T(1024)(128)(4,1)S(1)} fusion(pred[4096]{0:T(1024)(128)(4,1)S(1)} %compare_reduce_fusion, pred[4096]{0:T(1024)(128)(4,1)S(1)} %compare_reduce_fusion.1, pred[4096]{0:T(1024)(128)(4,1)S(1)} %compare_reduce_fusion.2, pred[4096]{0:T(1024)(128)(4,1)S(1)} %compare_reduce_fusion.3, ...), kind=kLoop, calls=%fused_computation.99 | loop fusion | flops 106496 | bytes 122984 | tf_op jit(solution)/shard_map/eq | solution.py:121
  53.1 1.3 copy.38
  55.7 15.7 %reduce-window.6 = s32[32,8,128]{2,1,0:T(8,128)S(1)} reduce-window(s32[32,8,128]{2,1,0:T(8,128)} %fusion.37, s32[]{:T(128)} %copy.75), window={size=1x1x128 pad=0_0x0_0x127_0}, to_apply=%region_7.8 | reduce-window | flops 4161536 | bytes 262148 | tf_op jit(solution)/shard_map/reduce-window
  72.2 1.0 copy.44
  74.6 1.3 broadcast_multiply_fusion
  75.9 1.4 copy.41
  77.3 1.5 mul.85
  81.7 41.2 %all-gather.3.cloned.1.call-done = bf16[4096,256]{1,0:T(8,128)(2,1)} async-done(((bf16[128,256]{1,0:T(8,128)(2,1)}), bf16[4096,256]{1,0:T(8,128)(2,1)}) %all-gather.3.cloned.1.call-update) | async-done | bytes 2097168 | tf_op jit(solution)/shard_map/all_gather | solution.py:116
  122.9 4.0 reshape.358
  126.9 3.4 copy.37
  130.3 6.1 %all-to-all-done = bf16[32,128,256]{1,2,0:T(8,128)(2,1)S(1)} async-done(((bf16[32,128,256]{1,2,0:T(8,128)(2,1)}), bf16[32,128,256]{1,2,0:T(8,128)(2,1)S(1)}, u32[]{:S(2)}, u32[]{:S(2)}) %all-to-all-start) | async-done | bytes 2097184 | tf_op jit(solution)/shard_map/all_to_all | solution.py:15
  136.4 2.7 copy.36
  139.1 3.1 reshape_reshape_reshape.3
  142.2 3.0 copy.39
  145.3 23.7 %while.15 = (s32[]{:T(128)}, f32[2,8,128]{2,1,0:T(8,128)S(1)}, f32[2,8,128]{2,1,0:T(8,128)S(1)}, f32[2,8,128,128]{3,2,1,0:T(8,128)S(1)}, pred[8,512]{1,0:T(8,128...) while((s32[]{:T(128)}, f32[2,8,128]{2,1,0:T(8,128)S(1)}, ...), condition=%wide.region_6.7_spmd.clone, body=%wide.region_0.6_spmd.clone.sunk | while | flops 551227520 | bytes 16131831 | solution.py:70
  147.6 5.4 conditional.3
  147.6 1.7 fusion.2
  150.3 2.6 fusion.8
  169.9 35.4 %all-gather.5.cloned.1.call-done = bf16[2048,1024]{1,0:T(8,128)(2,1)} async-done(((bf16[64,1024]{1,0:T(8,128)(2,1)}), bf16[2048,1024]{1,0:T(8,128)(2,1)}) %all-gather.5.cloned.1.call-update) | async-done | bytes 4194320 | tf_op jit(solution)/shard_map/all_gather | solution.py:132
  205.3 3.0 multiply_reduce_fusion
  209.1 14.9 %scatter_custom_fusion = bf16[1536,1024]{1,0:T(8,128)(2,1)} fusion(s32[1024]{0:T(1024)S(1)} %bitcast.130, bf16[128,1024]{1,0:T(8,128)(2,1)S(1)} %get-tuple-element.206, s32[1024]{0:T(1024)S(1)} %broadcast_clamp_fusion.1, bf16[]{:T(256)} %constant.107.clone.1), kind=kCustom, calls=%fused_computation.34 | custom fusion | bytes 3145730 | tf_op jit(solution)/shard_map/scatter | solution.py:150
  224.0 154.0 %all_to_all.15 = bf16[32,48,1024]{2,1,0:T(8,128)(2,1)S(1)} all-to-all(bf16[32,48,1024]{2,1,0:T(8,128)(2,1)} %bitcast.117), channel_id=1, replica_groups=mesh['pack'=16,'seq'=32] {'seq'}, dimensions={0} | all-to-all | bytes 6291456 | tf_op jit(solution)/shard_map/all_to_all | solution.py:153
  378.0 1.7 copy-done.1
  379.7 3.3 fusion.31
  383.0 7.8 %convolution_convert_fusion = bf16[1536,1024]{1,0:T(8,128)(2,1)} fusion(bf16[1536,1024]{1,0:T(8,128)(2,1)} %bitcast.120, f32[1536,384]{1,0:T(8,128)} %fusion.31, bf16[1,384,1024]{2,1,0:T(8,128)(2,1)S(1)} %copy-done, bf16[1,1024,384]{2,1,0:T(8,128)(2,1)S(1)} %copy-done.11), kind=kOutput, calls=%fused_computation.31 | convolution fusion | flops 2421030912 | bytes 10223616 | tf_op jit(solution)/shard_map/dot_general | solution.py:88
  390.8 4.9 all-to-all-start.2
  395.8 146.3 %all-to-all-done.2 = bf16[32,48,1024]{2,1,0:T(8,128)(2,1)} async-done(((bf16[32,48,1024]{2,1,0:T(8,128)(2,1)}), bf16[32,48,1024]{2,1,0:T(8,128)(2,1)}, u32[]{:S(2)}, u32[]{:S(2)}) %all-to-all-start.2) | async-done | bytes 3145760 | tf_op jit(solution)/shard_map/all_to_all | solution.py:155
  542.1 7.3 %gather_fusion = bf16[1024,1024]{1,0:T(8,128)(2,1)S(1)} fusion(bf16[1536,1024]{1,0:T(8,128)(2,1)} %bitcast.54, s32[1024]{0:T(1024)S(1)} %broadcast_clamp_fusion), kind=kCustom, calls=%fused_computation.1 | custom fusion | bytes 4198400 | tf_op jit(solution)/shard_map/gather | solution.py:156
  549.4 2.0 fusion.22
  (126 shorter events, 29.7 us)
Async XLA Ops:
  7.2 375.8 %copy-start = (bf16[1,384,1024]{2,1,0:T(8,128)(2,1)S(1)}, bf16[1,384,1024]{2,1,0:T(8,128)(2,1)}, u32[]{:S(2)}) copy-start(bf16[1,384,1024]{2,1,0:T(8,128)(2,1)} %param.24) | copy-start | bytes 2359300
  7.2 115.7 %all-gather.3.cloned.1.call-start = ((), (), s32[]{:S(2)}) async-start(), calls=%async_computation.3 | async-start | bytes 2162688 | tf_op jit(solution)/shard_map/all_gather | solution.py:116
  8.9 18.2 %copy-start.7 = (s32[128,8]{0,1:T(8,128)S(1)}, s32[128,8]{0,1:T(8,128)}, u32[]{:S(2)}) copy-start(s32[128,8]{0,1:T(8,128)} %param.25) | copy-start | bytes 12292
  8.9 20.5 %copy-start.3 = (s32[32]{0:T(128)S(1)}, s32[32]{0:T(128)}, u32[]{:S(2)}) copy-start(s32[32]{0:T(128)} %param.27) | copy-start | bytes 388
  8.9 43.2 %copy-start.4 = (bf16[128,2048]{1,0:T(8,128)(2,1)S(1)}, bf16[128,2048]{1,0:T(8,128)(2,1)}, u32[]{:S(2)}) copy-start(bf16[128,2048]{1,0:T(8,128)(2,1)} %param.16) | copy-start | bytes 1572868
  10.7 43.8 %copy-start.9 = (bf16[1024]{0:T(1024)(128)(2,1)S(1)}, bf16[1024]{0:T(1024)(128)(2,1)}, u32[]{:S(2)}) copy-start(bf16[1024]{0:T(1024)(128)(2,1)} %param.21) | copy-start | bytes 6148
  10.7 125.7 %all-to-all-start = ((bf16[32,128,256]{1,2,0:T(8,128)(2,1)}), bf16[32,128,256]{1,2,0:T(8,128)(2,1)S(1)}, u32[]{:S(2)}, u32[]{:S(2)}) async-start(bf16[32,128,256]{1,2,0:T(8,128)(2,1)} %stack.2), calls=%async_computation | async-start | bytes 4194304 | tf_op jit(solution)/shard_map/all_to_all | solution.py:15
  26.3 179.0 %all-gather.5.cloned.1.call-start = ((), (), s32[]{:S(2)}) async-start(), calls=%async_computation.4 | async-start | bytes 4325376 | tf_op jit(solution)/shard_map/all_gather | solution.py:132
  169.0 36.3 %copy-start.5 = (bf16[128,1024]{1,0:T(8,128)(2,1)S(1)}, bf16[128,1024]{1,0:T(8,128)(2,1)}, u32[]{:S(2)}) copy-start(bf16[128,1024]{1,0:T(8,128)(2,1)} %param.19) | copy-start | bytes 786436
  169.7 38.6 %copy-start.6 = (f32[1024]{0:T(1024)S(1)}, f32[1024]{0:T(1024)}, u32[]{:S(2)}) copy-start(f32[1024]{0:T(1024)} %convert_element_type.59) | copy-start | bytes 12292
  169.9 39.2 %copy-start.2 = (bf16[16,8,16,128]{3,1,2,0:T(8,128)(2,1)}, bf16[16,8,16,128]{3,1,2,0:T(8,128)(2,1)S(1)}, u32[]{:S(2)}) copy-start(bf16[16,8,16,128]{3,1,2,0:T(8,128)(2,1)S(1)} %copy.56) | copy-start | bytes 1572868
  224.0 155.7 %copy-start.10 = (bf16[1,1024,384]{2,1,0:T(8,128)(2,1)S(1)}, bf16[1,1024,384]{2,1,0:T(8,128)(2,1)}, u32[]{:S(2)}) copy-start(bf16[1,1024,384]{2,1,0:T(8,128)(2,1)} %param.22) | copy-start | bytes 2359300
  378.0 1.7 copy-start.1
  379.7 3.3 copy-start.11
  390.8 5.0 copy-start.8
  390.8 151.3 %all-to-all-start.2 = ((bf16[32,48,1024]{2,1,0:T(8,128)(2,1)}), bf16[32,48,1024]{2,1,0:T(8,128)(2,1)}, u32[]{:S(2)}, u32[]{:S(2)}) async-start(bf16[32,48,1024]{2,1,0:T(8,128)(2,1)} %bitcast.118), calls=%async_computation.2 | async-start | bytes 6291456 | tf_op jit(solution)/shard_map/all_to_all | solution.py:155
Sparse Core Ops, SparseCore 0:
  10.1 112.7 all-gather.2
  125.0 80.2 all-gather.4
